TPU v7x, 32 devices: a whole 2x2x4 slice. The times are simulated.
32 devices in a mesh: group: 4 (over y, x), shard: 8 (over z, core).
Axes of the slice: x: 2, y: 2, z: 4, core: 2. Of those that a mesh axis runs over, the one named last changes fastest.
Arguments:
- entity: float32 [16384, 400], P(('group', 'shard')), may hold values from -6 to 6
- entity_state: float32 [16384], P(('group', 'shard')), may hold values from 0.1 to 10
- relation: float32 [1345, 400], replicated, may hold values from -6 to 6
- relation_state: float32 [1345], replicated, may hold values from 10 to 1000
- src_send: int32 [32, 8, 128], P(('group', 'shard')), may hold values from 0 to 511
- dst_send: int32 [32, 8, 128], P(('group', 'shard')), may hold values from 0 to 511
- edge_source: int32 [32768], P(('group', 'shard')), may hold values from 0 to 1023
- edge_relation: int32 [32768], P(('group', 'shard')), may hold values from 0 to 1344
- edge_target: int32 [32768], P(('group', 'shard')), may hold values from 0 to 1023
- neg_slots: int32 [64, 1000], P(('group', 'shard')), may hold values from 0 to 1023
- edge_count: int32 [32], P(('group', 'shard')), may hold values from 1 to 1024, 10922 in all
Outputs:
- entity_new: float32 [16384, 400], P(('group', 'shard'))
- relation_new: float32 [1345, 400], replicated
- edge_loss: float32 [32768], P(('group', 'shard'))
Inputs may be any that keep to these rules, and one draw needn't show every extreme that they name: The live edges of a device are its first edge_count slots; some device has all 1024 live.
All inputs are finite; a program needn't handle non-finite values.
Results may differ from a plain program's by a relative error of at most 0.0003.
Values sent between devices are 32-bit elements; how exact they have to be, the bound alone decides.
No kernel may reach another device: no remote copies, remote signals or barrier semaphores. Data moves between devices by JAX's collectives and lax.ppermute only.
A program may use at most 128 MiB of HBM per device.

v0:
```python
import jax
import jax.numpy as jnp
from jax import lax
from jax.sharding import PartitionSpec as P

SPAN = 512
learn_rate = 0.5


def passed_along(value, axis, by):
    count = lax.axis_size(axis)
    return lax.ppermute(value, axis, [(i, (i + by) % count) for i in range(count)])


def complex_product(multiplier, multiplicand):
    half_width = multiplier.shape[1] // 2
    first_real, first_imag = (multiplier[:, :half_width], multiplier[:, half_width:])
    second_real, second_imag = (multiplicand[:, :half_width], multiplicand[:, half_width:])
    return jnp.concatenate(
        [
            first_real * second_real - first_imag * second_imag,
            first_real * second_imag + first_imag * second_real,
        ],
        axis=1,
    )


def conj_product(multiplier, multiplicand):
    half_width = multiplier.shape[1] // 2
    first_real, first_imag = (multiplier[:, :half_width], multiplier[:, half_width:])
    second_real, second_imag = (multiplicand[:, :half_width], multiplicand[:, half_width:])
    return jnp.concatenate(
        [
            first_real * second_real + first_imag * second_imag,
            first_imag * second_real - first_real * second_imag,
        ],
        axis=1,
    )


def span_terms(queries, tail_rows, negatives, live_mask):
    pos_score = jnp.sum(queries * tail_rows, axis=1)
    neg_score = jnp.dot(queries, negatives.T, precision=lax.Precision.HIGHEST)
    score_peak = jnp.maximum(pos_score, jnp.max(neg_score, axis=1))
    exp_total = jnp.exp(pos_score - score_peak) + jnp.sum(
        jnp.exp(neg_score - score_peak[:, None]), axis=1
    )
    log_total = score_peak + jnp.log(exp_total)
    edge_loss = (log_total - pos_score) * live_mask
    pos_grad = (jnp.exp(pos_score - log_total) - 1.0) * live_mask
    neg_grad = jnp.exp(neg_score - log_total[:, None]) * live_mask[:, None]
    neg_query = jnp.dot(neg_grad, negatives, precision=lax.Precision.HIGHEST)
    negative_grad = lax.dot_general(
        neg_grad, queries, (((0,), (0,)), ((), ())), precision=lax.Precision.HIGHEST
    )
    return (edge_loss, pos_grad, neg_query, negative_grad)


def adagrad(params, accumulator, gradient):
    new_state = accumulator + jnp.mean(gradient * gradient, axis=1)
    return params - learn_rate * gradient / jnp.sqrt(new_state)[:, None]


def on_device(
    entity,
    entity_state,
    relation,
    relation_state,
    src_send,
    dst_send,
    edge_source,
    edge_relation,
    edge_target,
    neg_slots,
    edge_count,
):
    feature_count = entity.shape[1]
    peer_count, block_size = (src_send.shape[1], src_send.shape[2])
    table_rows = peer_count * block_size
    edge_rows = edge_source.shape[0]
    spans = edge_rows // SPAN
    sent_source = lax.all_to_all(
        entity[src_send[0]], "shard", split_axis=0, concat_axis=0, tiled=True
    )
    source_table = sent_source.reshape(table_rows, feature_count)
    shifted = passed_along(entity[dst_send[0]], "group", -1)
    target_blocks = lax.all_to_all(shifted, "shard", split_axis=0, concat_axis=0, tiled=True)
    target_table = target_blocks.reshape(table_rows, feature_count)
    live_count = edge_count[0]
    live_mask = (jnp.arange(edge_rows, dtype=jnp.int32) < live_count).astype(jnp.float32)
    head_rows = source_table[edge_source]
    tail_rows = target_table[edge_target]
    rel_rows = relation[edge_relation]
    queries = complex_product(head_rows, rel_rows)

    def span_turn(position, carried):
        loss_all, pos_all, query_all, target_grad = carried
        first_row = position * SPAN
        slots = neg_slots[position]
        edge_loss, pos_grad, neg_query, negative_grad = span_terms(
            lax.dynamic_slice_in_dim(queries, first_row, SPAN),
            lax.dynamic_slice_in_dim(tail_rows, first_row, SPAN),
            target_table[slots],
            lax.dynamic_slice_in_dim(live_mask, first_row, SPAN),
        )
        loss_all = lax.dynamic_update_slice_in_dim(loss_all, edge_loss, first_row, 0)
        pos_all = lax.dynamic_update_slice_in_dim(pos_all, pos_grad, first_row, 0)
        query_all = lax.dynamic_update_slice_in_dim(query_all, neg_query, first_row, 0)
        target_grad = target_grad.at[slots].add(negative_grad)
        return (loss_all, pos_all, query_all, target_grad)

    initial = (
        jnp.zeros((edge_rows,), jnp.float32),
        jnp.zeros((edge_rows,), jnp.float32),
        jnp.zeros((edge_rows, feature_count), jnp.float32),
        jnp.zeros((table_rows, feature_count), jnp.float32),
    )
    edge_loss, pos_grad, neg_query, target_grad = lax.fori_loop(0, spans, span_turn, initial)
    query_grad = pos_grad[:, None] * tail_rows + neg_query
    target_grad = target_grad.at[edge_target].add(pos_grad[:, None] * queries)
    source_grad = (
        jnp.zeros((table_rows, feature_count), jnp.float32)
        .at[edge_source]
        .add(conj_product(query_grad, rel_rows))
    )
    relation_part = (
        jnp.zeros(relation.shape, jnp.float32)
        .at[edge_relation]
        .add(conj_product(query_grad, head_rows))
    )
    relation_total = lax.psum(relation_part, ("group", "shard"))
    returned_source = lax.all_to_all(
        source_grad.reshape(peer_count, block_size, feature_count),
        "shard",
        split_axis=0,
        concat_axis=0,
        tiled=True,
    )
    entity_grad = (
        jnp.zeros(entity.shape, jnp.float32)
        .at[src_send[0].reshape(-1)]
        .add(returned_source.reshape(-1, feature_count))
    )
    target_blocks_grad = target_grad.reshape(peer_count, block_size, feature_count)
    returned_blocks = lax.all_to_all(
        target_blocks_grad, "shard", split_axis=0, concat_axis=0, tiled=True
    )
    home_blocks = passed_along(returned_blocks, "group", 1)
    entity_grad = entity_grad.at[dst_send[0].reshape(-1)].add(
        home_blocks.reshape(-1, feature_count)
    )
    return (
        adagrad(entity, entity_state, entity_grad),
        adagrad(relation, relation_state, relation_total),
        edge_loss,
    )


def solution(mesh):
    return jax.shard_map(
        on_device,
        mesh=mesh,
        in_specs=(
            P(("group", "shard"), None),
            P(("group", "shard")),
            P(),
            P(),
            P(("group", "shard"), None, None),
            P(("group", "shard"), None, None),
            P(("group", "shard")),
            P(("group", "shard")),
            P(("group", "shard")),
            P(("group", "shard"), None),
            P(("group", "shard")),
        ),
        out_specs=(P(("group", "shard"), None), P(), P(("group", "shard"))),
        check_vma=False,
    )
```

profile of v0, /device:TPU:0, one launch (start us, length us, event | category | flops | bytes accessed | tf_op | source)
XLA Modules:
  0.0 453.2 jit_solution(17644259954135910867)
XLA Ops:
  9.4 3.5 gather_fusion.1
  14.6 6.5 %all-to-all-start = ((f32[8,128,400]{1,2,0:T(8,128)}), f32[8,128,400]{1,2,0:T(8,128)}, u32[]{:S(2)}, u32[]{:S(2)}) async-start(f32[8,128,400]{1,2,0:T(8,128)} %copy.47), calls=%async_computation | async-start | bytes 3276800 | tf_op jit(solution)/shard_map/all_to_all | solution.py:82
  21.1 3.5 gather_fusion.4
  28.8 36.1 %collective-permute-done = f32[8,128,400]{1,2,0:T(8,128)} collective-permute-done((f32[8,128,400]{1,2,0:T(8,128)}, f32[8,128,400]{1,2,0:T(8,128)}, u32[]{:S(2)}, u32[]{:S(2)}) %collective-permute-start) | collective-permute-done | bytes 1638432 | tf_op jit(solution)/shard_map/ppermute | solution.py:12
  64.9 4.7 %all-to-all-start.1 = ((f32[8,128,400]{1,2,0:T(8,128)}), f32[8,128,400]{1,2,0:T(8,128)}, u32[]{:S(2)}, u32[]{:S(2)}) async-start(f32[8,128,400]{1,2,0:T(8,128)} %collective-permute-done), calls=%async_computation.1 | async-start | bytes 3276800 | tf_op jit(solution)/shard_map/all_to_all | solution.py:87
  72.9 4.9 %gather_fusion.3 = f32[1024,400]{1,0:T(8,128)} fusion(f32[1345,400]{1,0:T(8,128)S(1)} %copy.49, s32[1024]{0:T(1024)S(1)} %get-tuple-element.335), kind=kCustom, calls=%fused_computation.3 | custom fusion | bytes 3280896 | tf_op jit(solution)/shard_map/gather | solution.py:93
  79.6 4.9 %gather_fusion.2 = f32[1024,400]{1,0:T(8,128)} fusion(f32[1024,400]{1,0:T(8,128)S(1)} %bitcast.42, s32[1024]{0:T(1024)S(1)} %get-tuple-element.338), kind=kCustom, calls=%fused_computation.2 | custom fusion | bytes 3280896 | tf_op jit(solution)/shard_map/gather | solution.py:91
  84.6 3.1 multiply_subtract_fusion.2
  90.5 18.4 %all-to-all-done.1 = f32[8,128,400]{1,2,0:T(8,128)} async-done(((f32[8,128,400]{1,2,0:T(8,128)}), f32[8,128,400]{1,2,0:T(8,128)}, u32[]{:S(2)}, u32[]{:S(2)}) %all-to-all-start.1) | async-done | bytes 1638432 | tf_op jit(solution)/shard_map/all_to_all | solution.py:87
  110.8 4.9 %gather_fusion.5 = f32[1024,400]{1,0:T(8,128)} fusion(f32[1024,400]{1,0:T(8,128)S(1)} %bitcast.39, s32[1024]{0:T(1024)S(1)} %get-tuple-element.337), kind=kCustom, calls=%fused_computation.5 | custom fusion | bytes 3280896 | tf_op jit(solution)/shard_map/gather | solution.py:92
  118.7 68.8 %while.21 = (s32[]{:T(128)}, f32[1024]{0:T(1024)S(1)}, f32[1024]{0:T(1024)S(1)}, f32[1024,400]{0,1:T(8,128)}, f32[1024,400]{1,0:T(8,128)}, /*index=5*/f32[1024,4...) while((s32[]{:T(128)}, f32[1024]{0:T(1024)S(1)}, ...), condition=%wide.region_5.0_spmd, body=%wide.region_0.0_spmd.sunk | while | flops 7377200640 | bytes 52573032 | solution.py:118
  120.9 4.9 %gather_fusion = f32[1000,400]{1,0:T(8,128)} fusion(f32[1024,400]{1,0:T(8,128)S(1)} %get-tuple-element.447, s32[1024]{0:T(1024)S(1)} %pad_clamp_fusion.2), kind=kCustom, calls=%fused_computation.clone.1 | custom fusion | bytes 3204000 | tf_op jit(solution)/shard_map/while/body/eval_jaxpr/gather | solution.py:103
  125.8 5.4 %fusion.44 = (f32[512]{0:T(512)S(1)}, f32[512,1000]{0,1:T(8,128)S(1)}) fusion(f32[1000,400]{1,0:T(8,128)} %gather_fusion, f32[1024,400]{1,0:T(8,128)} %get-tuple-element.444, s32[]{:T(128)S(6)} %select_n.125), kind=kOutput, calls=%fused_computation.77.clone.1 | convolution fusion | flops 2458111488 | bytes 5146628 | tf_op jit(solution)/shard_map/while/body/eval_jaxpr/dot_general | solution.py:43
  132.8 4.2 fusion.45
  138.3 4.9 %fusion.46 = f32[1000,400]{1,0:T(8,128)} fusion(f32[512,1000]{0,1:T(8,128)S(1)} %get-tuple-element.407, f32[512]{0:T(512)S(1)} %get-tuple-element.408, f32[512]{0:T(512)S(1)} %get-tuple-element.409, f32[1024,400]{1,0:T(8,128)S(1)} %copy-done.5, s32[]{:T(128)S(6)} %select_n.125), kind=kOutput, calls=%fused_computation.14.clone.1 | convolution fusion | flops 2458624000 | bytes 4700676 | tf_op jit(solution)/shard_map/while/body/eval_jaxpr/dot_general | solution.py:53
  143.2 10.1 %scatter_fusion = f32[1024,400]{1,0:T(8,128)} fusion(f32[1024,400]{1,0:T(8,128)} %get-tuple-element.429, s32[1000]{0:T(1024)S(1)} %bitcast.49, f32[1000,400]{1,0:T(8,128)} %fusion.46), kind=kCustom, calls=%fused_computation.6.clone.1 | custom fusion | flops 400000 | bytes 4804000 | tf_op jit(solution)/shard_map/while/body/eval_jaxpr/scatter-add | solution.py:109
  155.0 4.9 %gather_fusion = f32[1000,400]{1,0:T(8,128)} fusion(f32[1024,400]{1,0:T(8,128)S(1)} %get-tuple-element.447, s32[1024]{0:T(1024)S(1)} %pad_clamp_fusion.2), kind=kCustom, calls=%fused_computation.clone.1 | custom fusion | bytes 3204000 | tf_op jit(solution)/shard_map/while/body/eval_jaxpr/gather | solution.py:103
  159.9 5.4 %fusion.44 = (f32[512]{0:T(512)S(1)}, f32[512,1000]{0,1:T(8,128)S(1)}) fusion(f32[1000,400]{1,0:T(8,128)} %gather_fusion, f32[1024,400]{1,0:T(8,128)} %get-tuple-element.444, s32[]{:T(128)S(6)} %select_n.125), kind=kOutput, calls=%fused_computation.77.clone.1 | convolution fusion | flops 2458111488 | bytes 5146628 | tf_op jit(solution)/shard_map/while/body/eval_jaxpr/dot_general | solution.py:43
  166.9 4.2 fusion.45
  172.4 4.9 %fusion.46 = f32[1000,400]{1,0:T(8,128)} fusion(f32[512,1000]{0,1:T(8,128)S(1)} %get-tuple-element.407, f32[512]{0:T(512)S(1)} %get-tuple-element.408, f32[512]{0:T(512)S(1)} %get-tuple-element.409, f32[1024,400]{1,0:T(8,128)S(1)} %copy-done.5, s32[]{:T(128)S(6)} %select_n.125), kind=kOutput, calls=%fused_computation.14.clone.1 | convolution fusion | flops 2458624000 | bytes 4700676 | tf_op jit(solution)/shard_map/while/body/eval_jaxpr/dot_general | solution.py:53
  177.2 10.1 %scatter_fusion = f32[1024,400]{1,0:T(8,128)} fusion(f32[1024,400]{1,0:T(8,128)} %get-tuple-element.429, s32[1000]{0:T(1024)S(1)} %bitcast.49, f32[1000,400]{1,0:T(8,128)} %fusion.46), kind=kCustom, calls=%fused_computation.6.clone.1 | custom fusion | flops 400000 | bytes 4804000 | tf_op jit(solution)/shard_map/while/body/eval_jaxpr/scatter-add | solution.py:109
  187.5 10.6 %scatter_custom_fusion.3 = f32[1024,400]{1,0:T(8,128)} fusion(f32[1024,400]{1,0:T(8,128)} %get-tuple-element.250, s32[1024]{0:T(1024)S(1)} %get-tuple-element.336, f32[1024]{0:T(1024)S(1)} %get-tuple-element.248, f32[1024,200]{1,0:T(8,128)} %copy-done.9, f32[1024,200]{1,0:T(8,128)S(1)} %get-tuple-element.330), kind=kCustom, calls=%fused_computation.43 | custom fusion | flops 1228800 | bytes 3739648 | tf_op jit(solution)/shard_map/scatter-add | solution.py:120
  200.9 4.3 all-to-all-start.3
  213.6 8.1 %scatter_custom_fusion.1 = f32[1024,400]{1,0:T(8,128)S(1)} fusion(s32[1024]{0:T(1024)S(1)} %get-tuple-element.339, f32[1024,200]{1,0:T(8,128)S(1)} %get-tuple-element.332, f32[]{:T(128)} %constant.108, f32[1024,200]{1,0:T(8,128)} %get-tuple-element.333, f32[]{:T(128)} %constant.97.clone.1), kind=kCustom, calls=%fused_computation.35 | custom fusion | flops 819200 | bytes 3506184 | tf_op jit(solution)/shard_map/scatter-add | solution.py:124
  223.5 21.0 %all-to-all-done.3 = f32[8,128,400]{1,2,0:T(8,128)} async-done(((f32[8,128,400]{1,2,0:T(8,128)}), f32[8,128,400]{1,2,0:T(8,128)}, u32[]{:S(2)}, u32[]{:S(2)}) %all-to-all-start.3) | async-done | bytes 1638432 | tf_op jit(solution)/shard_map/all_to_all | solution.py:145
  244.4 4.3 all-to-all-start.2
  248.8 9.0 %scatter_custom_fusion.5 = f32[1345,400]{1,0:T(8,128)} fusion(s32[1024]{0:T(1024)S(1)} %get-tuple-element.334, f32[1024,200]{1,0:T(8,128)S(1)} %copy-done.13, f32[]{:T(128)} %constant.108, f32[1024,200]{1,0:T(8,128)S(1)} %copy-done.12, f32[]{:T(128)} %constant.97.clone.1), kind=kCustom, calls=%fused_computation.39 | custom fusion | flops 819200 | bytes 4249160 | tf_op jit(solution)/shard_map/scatter-add | solution.py:129
  260.3 155.8 %all-reduce.2.cloned.1.call-done = f32[1345,400]{1,0:T(8,128)} async-done(((f32[1345,400]{1,0:T(8,128)}), f32[1345,400]{1,0:T(8,128)}) %all-reduce.2.cloned.1.call-update) | async-done | bytes 2152016 | tf_op jit(solution)/shard_map/psum | solution.py:131
  418.2 3.8 divide_subtract_fusion
  422.0 3.3 copy.65
  427.1 6.8 %scatter_custom_fusion.2 = f32[512,400]{1,0:T(8,128)S(1)} fusion(s32[1024]{0:T(1024)S(1)} %bitcast.53, f32[1024,400]{1,0:T(8,128)S(1)} %bitcast.47, f32[]{:T(128)} %constant.97.clone.1), kind=kCustom, calls=%fused_computation.57 | custom fusion | flops 409600 | bytes 819204 | tf_op jit(solution)/shard_map/scatter-add | solution.py:142
  436.8 7.8 %scatter_fusion.1 = f32[512,400]{1,0:T(8,128)S(1)} fusion(f32[512,400]{1,0:T(8,128)S(1)} %scatter_custom_fusion.2, s32[1024]{0:T(1024)S(1)} %bitcast.50, f32[1024,400]{1,0:T(8,128)} %bitcast.43), kind=kCustom, calls=%fused_computation.10 | custom fusion | flops 409600 | bytes 4919296 | tf_op jit(solution)/shard_map/scatter-add | solution.py:149
  (107 shorter events, 53.1 us)
Async XLA Ops:
  8.6 12.5 %copy-start = (f32[512,400]{1,0:T(8,128)}, f32[512,400]{1,0:T(8,128)S(1)}, u32[]{:S(2)}) copy-start(f32[512,400]{1,0:T(8,128)S(1)} %copy.62) | copy-start | bytes 2457604
  14.6 6.5 %copy-start.16 = (s32[1,8,128]{2,1,0:T(8,128)S(1)}, s32[1,8,128]{2,1,0:T(8,128)}, u32[]{:S(2)}) copy-start(s32[1,8,128]{2,1,0:T(8,128)} %param.18) | copy-start | bytes 12292
  14.6 50.3 %all-to-all-start = ((f32[8,128,400]{1,2,0:T(8,128)}), f32[8,128,400]{1,2,0:T(8,128)}, u32[]{:S(2)}, u32[]{:S(2)}) async-start(f32[8,128,400]{1,2,0:T(8,128)} %copy.47), calls=%async_computation | async-start | bytes 3276800 | tf_op jit(solution)/shard_map/all_to_all | solution.py:82
  26.4 38.5 %collective-permute-start = (f32[8,128,400]{1,2,0:T(8,128)}, f32[8,128,400]{1,2,0:T(8,128)}, u32[]{:S(2)}, u32[]{:S(2)}) collective-permute-start(f32[8,128,400]{1,2,0:T(8,128)} %copy.51), channel_id=1, source_target_pairs={{0,24},{8,0},{16,8},{24,16},{1,25},{9,1},{17,9},{25,17},{2,26},{10... | collective-permute-start | bytes 4915208 | tf_op jit(solution)/shard_map/ppermute | solution.py:12
  64.9 44.0 %all-to-all-start.1 = ((f32[8,128,400]{1,2,0:T(8,128)}), f32[8,128,400]{1,2,0:T(8,128)}, u32[]{:S(2)}, u32[]{:S(2)}) async-start(f32[8,128,400]{1,2,0:T(8,128)} %collective-permute-done), calls=%async_computation.1 | async-start | bytes 3276800 | tf_op jit(solution)/shard_map/all_to_all | solution.py:87
  69.6 3.2 copy-start.18
  72.1 5.6 %copy-start.3 = (f32[1345,400]{1,0:T(8,128)}, f32[1345,400]{1,0:T(8,128)S(1)}, u32[]{:S(2)}) copy-start(f32[1345,400]{1,0:T(8,128)S(1)} %copy.49) | copy-start | bytes 6456004
  72.8 4.9 %copy-start.19 = (s32[1024]{0:T(1024)S(1)}, s32[1024]{0:T(1024)}, u32[]{:S(2)}) copy-start(s32[1024]{0:T(1024)} %param.19) | copy-start | bytes 12292
  72.8 4.9 %copy-start.20 = (s32[1024]{0:T(1024)S(1)}, s32[1024]{0:T(1024)}, u32[]{:S(2)}) copy-start(s32[1024]{0:T(1024)} %param.21) | copy-start | bytes 12292
  115.6 3.1 copy-start.14
  125.8 6.1 %copy-start.10 = (f32[1024,400]{0,1:T(8,128)S(1)}, f32[1024,400]{0,1:T(8,128)}, u32[]{:S(2)}) copy-start(f32[1024,400]{0,1:T(8,128)} %get-tuple-element.428) | copy-start | bytes 4915204 | tf_op jit(solution)/shard_map/while
  131.2 1.6 copy-start.2
  132.8 5.5 %copy-start.5 = (f32[1024,400]{1,0:T(8,128)S(1)}, f32[1024,400]{1,0:T(8,128)}, u32[]{:S(2)}) copy-start(f32[1024,400]{1,0:T(8,128)} %get-tuple-element.444) | copy-start | bytes 4915204 | tf_op jit(solution)/shard_map/while
  137.0 1.3 copy-start.11
  159.9 6.1 %copy-start.10 = (f32[1024,400]{0,1:T(8,128)S(1)}, f32[1024,400]{0,1:T(8,128)}, u32[]{:S(2)}) copy-start(f32[1024,400]{0,1:T(8,128)} %get-tuple-element.428) | copy-start | bytes 4915204 | tf_op jit(solution)/shard_map/while
  165.3 1.6 copy-start.2
  166.9 5.5 %copy-start.5 = (f32[1024,400]{1,0:T(8,128)S(1)}, f32[1024,400]{1,0:T(8,128)}, u32[]{:S(2)}) copy-start(f32[1024,400]{1,0:T(8,128)} %get-tuple-element.444) | copy-start | bytes 4915204 | tf_op jit(solution)/shard_map/while
  187.5 10.6 %copy-start.21 = (f32[1024]{0:T(1024)}, f32[1024]{0:T(1024)S(1)}, u32[]{:S(2)}) copy-start(f32[1024]{0:T(1024)S(1)} %get-tuple-element.300) | copy-start | bytes 12292
  200.9 43.5 %all-to-all-start.3 = ((f32[8,128,400]{1,2,0:T(8,128)}), f32[8,128,400]{1,2,0:T(8,128)}, u32[]{:S(2)}, u32[]{:S(2)}) async-start(f32[8,128,400]{1,2,0:T(8,128)} %copy.59), calls=%async_computation.3 | async-start | bytes 3276800 | tf_op jit(solution)/shard_map/all_to_all | solution.py:145
  205.2 3.0 copy-start.6
  208.2 2.2 copy-start.7
  208.2 2.9 copy-start.8
  223.5 25.3 %copy-start.12 = (f32[1024,200]{1,0:T(8,128)S(1)}, f32[1024,200]{1,0:T(8,128)}, u32[]{:S(2)}) copy-start(f32[1024,200]{1,0:T(8,128)} %get-tuple-element.326) | copy-start | bytes 2457604
  223.5 25.3 %copy-start.13 = (f32[1024,200]{1,0:T(8,128)S(1)}, f32[1024,200]{1,0:T(8,128)}, u32[]{:S(2)}) copy-start(f32[1024,200]{1,0:T(8,128)} %get-tuple-element.327) | copy-start | bytes 2457604
  244.4 180.8 %all-to-all-start.2 = ((f32[8,128,400]{1,2,0:T(8,128)}), f32[8,128,400]{1,2,0:T(8,128)}, u32[]{:S(2)}, u32[]{:S(2)}) async-start(f32[8,128,400]{1,2,0:T(8,128)} %copy.55), calls=%async_computation.2 | async-start | bytes 3276800 | tf_op jit(solution)/shard_map/all_to_all | solution.py:132
  248.7 167.4 %all-reduce.2.cloned.1.call-start = ((), (), s32[]{:S(2)}) async-start(), calls=%async_computation.4 | async-start | bytes 5537792 | tf_op jit(solution)/shard_map/psum | solution.py:131
  257.8 2.5 copy-start.15
  257.8 160.4 %copy-start.17 = (f32[1345]{0:T(1024)S(1)}, f32[1345]{0:T(1024)}, u32[]{:S(2)}) copy-start(f32[1345]{0:T(1024)} %param.16) | copy-start | bytes 16144
  257.8 160.4 %copy-start.4 = (f32[1345,400]{1,0:T(8,128)S(1)}, f32[1345,400]{1,0:T(8,128)}, u32[]{:S(2)}) copy-start(f32[1345,400]{1,0:T(8,128)} %copy-done.3) | copy-start | bytes 6456004
  257.8 176.1 %collective-permute-start.1 = (f32[8,128,400]{1,2,0:T(8,128)}, f32[8,128,400]{1,2,0:T(8,128)}, u32[]{:S(2)}, u32[]{:S(2)}) collective-permute-start(f32[8,128,400]{1,2,0:T(8,128)} %all-to-all-done.3), channel_id=1, source_target_pairs={{0,8},{8,16},{16,24},{24,0},{1,9},{9,17},{17,25},{25,1},{2,10},{10... | collective-permute-start | bytes 4915208 | tf_op jit(solution)/shard_map/ppermute | solution.py:12
  436.8 7.9 %copy-start.22 = (f32[512]{0:T(512)S(1)}, f32[512]{0:T(512)}, u32[]{:S(2)}) copy-start(f32[512]{0:T(512)} %param.14) | copy-start | bytes 6148
  436.8 7.9 %copy-start.1 = (f32[512,400]{1,0:T(8,128)S(1)}, f32[512,400]{1,0:T(8,128)}, u32[]{:S(2)}) copy-start(f32[512,400]{1,0:T(8,128)} %copy-done) | copy-start | bytes 2457604
  (2 other events, 2.3 us)
Sparse Core Ops, SparseCore 0:
  257.9 158.1 all-reduce.1
where the time goes:
time: 458 us; the launch traced here: 453 us
  waiting for transfers between devices  231 us (50%)
  other arithmetic  83.6 us (18%)
  local copies, waits for them, and re-layouts  68.6 us (15%)
  matrix products  29 us (6%)
  starting transfers between devices  24.7 us (5%)
  between operations  15.3 us (3%)
    psum x1, waiting for transfers between devices, on_device(): relation_total = lax.psum(relation_part, ('group', 'shard'))  156 us
    ppermute x2, waiting for transfers between devices, passed_along(): lax.ppermute(value, axis, [(i, (i + by) % count) for i in range(count)])  36.1 us
    all_to_all x1, waiting for transfers between devices, on_device(): lax.all_to_all(target_blocks_grad, 'shard', split_axis=0, concat_axis=0,...  21 us
    scatter-add x2, other arithmetic, span_turn(): target_grad = target_grad.at[slots].add(negative_grad)  20.2 us
    all_to_all x1, waiting for transfers between devices, on_device(): lax.all_to_all(shifted, 'shard', split_axis=0, concat_axis=0, tiled=True)  18.4 us
    dot_general x2, matrix products, span_terms(): neg_score = jnp.dot(queries, negatives.T, precision=lax.Precision.HIGHEST)  10.9 us
    scatter-add x1, other arithmetic, on_device(): target_grad = target_grad.at[edge_target].add(pos_grad[:, None] * queries)  10.6 us
    unnamed x42, local copies, waits for them, and re-layouts  10.4 us
  transfers between devices with their start and end apart: 7, of which 4 were waited for; matrix products, arithmetic and copies ran while one was open for 15% of the time, Pallas kernels for 0%

commit v1 on v0

--- a/solution.py
+++ b/solution.py
@@ -142,9 +142,15 @@
         .add(returned_source.reshape(-1, feature_count))
     )
     target_blocks_grad = target_grad.reshape(peer_count, block_size, feature_count)
-    returned_blocks = lax.all_to_all(
-        target_blocks_grad, "shard", split_axis=0, concat_axis=0, tiled=True
-    )
+    ways, here = (lax.axis_size("shard"), lax.axis_index("shard"))
+    width = target_blocks_grad.shape[0] // ways
+    turned = jnp.roll(target_blocks_grad, -here * width, axis=0)
+    got = [lax.slice_in_dim(turned, 0, width, axis=0)]
+    for far in range(1, ways):
+        sent = lax.slice_in_dim(turned, far * width, (far + 1) * width, axis=0)
+        got.append(lax.ppermute(sent, "shard", [(d, (d + far) % ways) for d in range(ways)]))
+    line = jnp.concatenate(got[::-1], axis=0)
+    returned_blocks = jnp.roll(line, (here + 1) * got[0].shape[0], axis=0)
     home_blocks = passed_along(returned_blocks, "group", 1)
     entity_grad = entity_grad.at[dst_send[0].reshape(-1)].add(
         home_blocks.reshape(-1, feature_count)

time: 458 us -> 462 us (level)
  waiting for transfers between devices: 231 us -> 200 us
  starting transfers between devices: 24.7 us -> 50.2 us
  local copies, waits for them, and re-layouts: 68.6 us -> 77.6 us
    psum x1, waiting for transfers between devices: 156 us -> 111 us  [on_device(): relation_total = lax.psum(relation_part, ('group', 'shard'))]
    ppermute x0 -> x7, waiting for transfers between devices: none -> 35.3 us  [on_device(): lax.ppermute(sent, 'shard', [(d, (d + far) % ways) for d in range(ways)])]
    ppermute x0 -> x7, starting transfers between devices: none -> 29.7 us  [on_device(): lax.ppermute(sent, 'shard', [(d, (d + far) % ways) for d in range(ways)])]
    all_to_all x1 -> x0, waiting for transfers between devices: 21 us -> none  [on_device(): lax.all_to_all(target_blocks_grad, 'shard', split_axis=0, concat_axis=0,...]
    concatenate x0 -> x1, local copies, waits for them, and re-layouts: none -> 6.13 us  [on_device(): line = jnp.concatenate(got[::-1], axis=0)]
    unnamed x42 -> x46, local copies, waits for them, and re-layouts: 10.4 us -> 11.9 us
  transfers between devices with their start and end apart: 7 -> 13, of which waited for: 4 -> 6; matrix products, arithmetic and copies ran while one was open for 15% -> 14% of each run, Pallas kernels for 0% -> 0%
where the time goes in v1:
time: 462 us; the launch traced here: 457 us
  waiting for transfers between devices  200 us (43%)
  other arithmetic  83.5 us (18%)
  local copies, waits for them, and re-layouts  77.6 us (17%)
  starting transfers between devices  50.2 us (11%)
  matrix products  29.2 us (6%)
  between operations  15.4 us (3%)
    psum x1, waiting for transfers between devices, on_device(): relation_total = lax.psum(relation_part, ('group', 'shard'))  111 us
    ppermute x2, waiting for transfers between devices, passed_along(): lax.ppermute(value, axis, [(i, (i + by) % count) for i in range(count)])  36.1 us
    ppermute x7, waiting for transfers between devices, on_device(): lax.ppermute(sent, 'shard', [(d, (d + far) % ways) for d in range(ways)])  35.3 us
    ppermute x7, starting transfers between devices, on_device(): lax.ppermute(sent, 'shard', [(d, (d + far) % ways) for d in range(ways)])  29.7 us
    scatter-add x2, other arithmetic, span_turn(): target_grad = target_grad.at[slots].add(negative_grad)  20.2 us
    all_to_all x1, waiting for transfers between devices, on_device(): lax.all_to_all(shifted, 'shard', split_axis=0, concat_axis=0, tiled=True)  18.4 us
    unnamed x46, local copies, waits for them, and re-layouts  11.9 us
    dot_general x2, matrix products, span_terms(): neg_score = jnp.dot(queries, negatives.T, precision=lax.Precision.HIGHEST)  10.9 us
  transfers between devices with their start and end apart: 13, of which 6 were waited for; matrix products, arithmetic and copies ran while one was open for 14% of the time, Pallas kernels for 0%

profile of v1, /device:TPU:0, one launch (start us, length us, event | category | flops | bytes accessed | tf_op | source)
XLA Modules:
  0.0 457.1 jit_solution(11899529721541960390)
XLA Ops:
  14.6 6.5 %all-to-all-start = ((f32[8,128,400]{1,2,0:T(8,128)}), f32[8,128,400]{1,2,0:T(8,128)}, u32[]{:S(2)}, u32[]{:S(2)}) async-start(f32[8,128,400]{1,2,0:T(8,128)} %copy.48), calls=%async_computation | async-start | bytes 3276800 | tf_op jit(solution)/shard_map/all_to_all | solution.py:82
  21.1 3.5 gather_fusion.4
  28.9 36.1 %collective-permute-done = f32[8,128,400]{1,2,0:T(8,128)} collective-permute-done((f32[8,128,400]{1,2,0:T(8,128)}, f32[8,128,400]{1,2,0:T(8,128)}, u32[]{:S(2)}, u32[]{:S(2)}) %collective-permute-start) | collective-permute-done | bytes 1638432 | tf_op jit(solution)/shard_map/ppermute | solution.py:12
  64.9 4.7 %all-to-all-start.1 = ((f32[8,128,400]{1,2,0:T(8,128)}), f32[8,128,400]{1,2,0:T(8,128)}, u32[]{:S(2)}, u32[]{:S(2)}) async-start(f32[8,128,400]{1,2,0:T(8,128)} %collective-permute-done), calls=%async_computation.1 | async-start | bytes 3276800 | tf_op jit(solution)/shard_map/all_to_all | solution.py:87
  72.9 4.9 %gather_fusion.3 = f32[1024,400]{1,0:T(8,128)} fusion(f32[1345,400]{1,0:T(8,128)S(1)} %copy.50, s32[1024]{0:T(1024)S(1)} %get-tuple-element.344), kind=kCustom, calls=%fused_computation.3 | custom fusion | bytes 3280896 | tf_op jit(solution)/shard_map/gather | solution.py:93
  79.7 4.9 %gather_fusion.2 = f32[1024,400]{1,0:T(8,128)} fusion(f32[1024,400]{1,0:T(8,128)S(1)} %bitcast.42, s32[1024]{0:T(1024)S(1)} %get-tuple-element.347), kind=kCustom, calls=%fused_computation.2 | custom fusion | bytes 3280896 | tf_op jit(solution)/shard_map/gather | solution.py:91
  90.6 18.4 %all-to-all-done.1 = f32[8,128,400]{1,2,0:T(8,128)} async-done(((f32[8,128,400]{1,2,0:T(8,128)}), f32[8,128,400]{1,2,0:T(8,128)}, u32[]{:S(2)}, u32[]{:S(2)}) %all-to-all-start.1) | async-done | bytes 1638432 | tf_op jit(solution)/shard_map/all_to_all | solution.py:87
  110.8 4.9 %gather_fusion.5 = f32[1024,400]{1,0:T(8,128)} fusion(f32[1024,400]{1,0:T(8,128)S(1)} %bitcast.39, s32[1024]{0:T(1024)S(1)} %get-tuple-element.346), kind=kCustom, calls=%fused_computation.5 | custom fusion | bytes 3280896 | tf_op jit(solution)/shard_map/gather | solution.py:92
  118.7 68.9 %while.21 = (s32[]{:T(128)}, f32[1024]{0:T(1024)S(1)}, f32[1024]{0:T(1024)S(1)}, f32[1024,400]{0,1:T(8,128)}, f32[1024,400]{1,0:T(8,128)}, /*index=5*/f32[1024,4...) while((s32[]{:T(128)}, f32[1024]{0:T(1024)S(1)}, ...), condition=%wide.region_5.0_spmd, body=%wide.region_0.0_spmd.sunk | while | flops 7377200640 | bytes 52573032 | solution.py:118
  121.0 4.9 %gather_fusion = f32[1000,400]{1,0:T(8,128)} fusion(f32[1024,400]{1,0:T(8,128)S(1)} %get-tuple-element.456, s32[1024]{0:T(1024)S(1)} %pad_clamp_fusion.2), kind=kCustom, calls=%fused_computation.clone.1 | custom fusion | bytes 3204000 | tf_op jit(solution)/shard_map/while/body/eval_jaxpr/gather | solution.py:103
  125.8 5.4 %fusion.47 = (f32[512]{0:T(512)S(1)}, f32[512,1000]{0,1:T(8,128)S(1)}) fusion(f32[1000,400]{1,0:T(8,128)} %gather_fusion, f32[1024,400]{1,0:T(8,128)} %get-tuple-element.453, s32[]{:T(128)S(6)} %select_n.141), kind=kOutput, calls=%fused_computation.83.clone.1 | convolution fusion | flops 2458111488 | bytes 5146628 | tf_op jit(solution)/shard_map/while/body/eval_jaxpr/dot_general | solution.py:43
  132.8 4.2 fusion.48
  138.2 5.0 %fusion.49 = f32[1000,400]{1,0:T(8,128)} fusion(f32[512,1000]{0,1:T(8,128)S(1)} %get-tuple-element.416, f32[512]{0:T(512)S(1)} %get-tuple-element.417, f32[512]{0:T(512)S(1)} %get-tuple-element.418, f32[1024,400]{1,0:T(8,128)S(1)} %copy-done.6, s32[]{:T(128)S(6)} %select_n.141), kind=kOutput, calls=%fused_computation.14.clone.1 | convolution fusion | flops 2458624000 | bytes 4700676 | tf_op jit(solution)/shard_map/while/body/eval_jaxpr/dot_general | solution.py:53
  143.2 10.1 %scatter_fusion = f32[1024,400]{1,0:T(8,128)} fusion(f32[1024,400]{1,0:T(8,128)} %get-tuple-element.438, s32[1000]{0:T(1024)S(1)} %bitcast.49, f32[1000,400]{1,0:T(8,128)} %fusion.49), kind=kCustom, calls=%fused_computation.6.clone.1 | custom fusion | flops 400000 | bytes 4804000 | tf_op jit(solution)/shard_map/while/body/eval_jaxpr/scatter-add | solution.py:109
  155.1 4.9 %gather_fusion = f32[1000,400]{1,0:T(8,128)} fusion(f32[1024,400]{1,0:T(8,128)S(1)} %get-tuple-element.456, s32[1024]{0:T(1024)S(1)} %pad_clamp_fusion.2), kind=kCustom, calls=%fused_computation.clone.1 | custom fusion | bytes 3204000 | tf_op jit(solution)/shard_map/while/body/eval_jaxpr/gather | solution.py:103
  159.9 5.4 %fusion.47 = (f32[512]{0:T(512)S(1)}, f32[512,1000]{0,1:T(8,128)S(1)}) fusion(f32[1000,400]{1,0:T(8,128)} %gather_fusion, f32[1024,400]{1,0:T(8,128)} %get-tuple-element.453, s32[]{:T(128)S(6)} %select_n.141), kind=kOutput, calls=%fused_computation.83.clone.1 | convolution fusion | flops 2458111488 | bytes 5146628 | tf_op jit(solution)/shard_map/while/body/eval_jaxpr/dot_general | solution.py:43
  166.9 4.2 fusion.48
  172.3 5.0 %fusion.49 = f32[1000,400]{1,0:T(8,128)} fusion(f32[512,1000]{0,1:T(8,128)S(1)} %get-tuple-element.416, f32[512]{0:T(512)S(1)} %get-tuple-element.417, f32[512]{0:T(512)S(1)} %get-tuple-element.418, f32[1024,400]{1,0:T(8,128)S(1)} %copy-done.6, s32[]{:T(128)S(6)} %select_n.141), kind=kOutput, calls=%fused_computation.14.clone.1 | convolution fusion | flops 2458624000 | bytes 4700676 | tf_op jit(solution)/shard_map/while/body/eval_jaxpr/dot_general | solution.py:53
  177.3 10.1 %scatter_fusion = f32[1024,400]{1,0:T(8,128)} fusion(f32[1024,400]{1,0:T(8,128)} %get-tuple-element.438, s32[1000]{0:T(1024)S(1)} %bitcast.49, f32[1000,400]{1,0:T(8,128)} %fusion.49), kind=kCustom, calls=%fused_computation.6.clone.1 | custom fusion | flops 400000 | bytes 4804000 | tf_op jit(solution)/shard_map/while/body/eval_jaxpr/scatter-add | solution.py:109
  196.3 8.3 %scatter_custom_fusion.1 = f32[1024,400]{1,0:T(8,128)S(1)} fusion(s32[1024]{0:T(1024)S(1)} %get-tuple-element.348, f32[1024,200]{1,0:T(8,128)} %get-tuple-element.333, f32[]{:T(128)} %constant.131, f32[1024,200]{1,0:T(8,128)} %get-tuple-element.334, f32[]{:T(128)} %constant.118.clone.1), kind=kCustom, calls=%fused_computation.39 | custom fusion | flops 819200 | bytes 3276808 | tf_op jit(solution)/shard_map/scatter-add | solution.py:124
  206.3 4.4 all-to-all-start.2
  210.8 8.5 %scatter_custom_fusion.3 = f32[1024,400]{1,0:T(8,128)S(1)} fusion(f32[1024,400]{1,0:T(8,128)S(1)} %copy-done, s32[1024]{0:T(1024)S(1)} %get-tuple-element.345, f32[1024]{0:T(1024)S(1)} %get-tuple-element.249, f32[1024,200]{1,0:T(8,128)} %copy-done.10, f32[1024,200]{1,0:T(8,128)S(1)} %get-tuple-element.331), kind=kCustom, calls=%fused_computation.47 | custom fusion | flops 1228800 | bytes 3510272 | tf_op jit(solution)/shard_map/scatter-add | solution.py:120
  221.3 9.3 %scatter_custom_fusion.5 = f32[1345,400]{1,0:T(8,128)} fusion(s32[1024]{0:T(1024)S(1)} %get-tuple-element.343, f32[1024,200]{1,0:T(8,128)} %get-tuple-element.328, f32[]{:T(128)} %constant.131, f32[1024,200]{1,0:T(8,128)S(1)} %copy-done.14, f32[]{:T(128)} %constant.118.clone.1), kind=kCustom, calls=%fused_computation.43 | custom fusion | flops 819200 | bytes 4019784 | tf_op jit(solution)/shard_map/scatter-add | solution.py:129
  240.0 5.6 %collective-permute-done.1 = f32[1,128,400]{1,0,2:T(1,128)S(1)} collective-permute-done((f32[1,128,400]{1,0,2:T(1,128)S(1)}, f32[1,128,400]{1,0,2:T(1,128)S(1)}, u32[]{:S(2)}, u32[]{:S(2)}) %collective-permute-start.1) | collective-permute-done | bytes 204832 | tf_op jit(solution)/shard_map/ppermute | solution.py:151
  245.6 11.1 %collective-permute-done.2 = f32[1,128,400]{1,0,2:T(1,128)S(1)} collective-permute-done((f32[1,128,400]{1,0,2:T(1,128)S(1)}, f32[1,128,400]{1,0,2:T(1,128)S(1)}, u32[]{:S(2)}, u32[]{:S(2)}) %collective-permute-start.2) | collective-permute-done | bytes 204832 | tf_op jit(solution)/shard_map/ppermute | solution.py:151
  256.7 23.2 %collective-permute-start.7 = (f32[1,128,400]{1,0,2:T(1,128)S(1)}, f32[1,128,400]{1,0,2:T(1,128)S(1)}, u32[]{:S(2)}, u32[]{:S(2)}) collective-permute-start(f32[1,128,400]{1,0,2:T(1,128)S(1)} %get-tuple-element.336), channel_id=1, source_target_pairs={{0,1},{1,2},{2,3},{3,4},{4,5},{5,6},{6,7},{7,0},{8,9},{9,10},{10,1... | collective-permute-start | bytes 614408 | tf_op jit(solution)/shard_map/ppermute | solution.py:151
  280.0 18.6 %collective-permute-done.4 = f32[1,128,400]{1,0,2:T(1,128)S(1)} collective-permute-done((f32[1,128,400]{1,0,2:T(1,128)S(1)}, f32[1,128,400]{1,0,2:T(1,128)S(1)}, u32[]{:S(2)}, u32[]{:S(2)}) %collective-permute-start.4) | collective-permute-done | bytes 204832 | tf_op jit(solution)/shard_map/ppermute | solution.py:151
  298.6 6.1 %concatenate.17 = f32[8,128,400]{1,0,2:T(8,128)S(1)} concatenate(f32[1,128,400]{1,0,2:T(1,128)S(1)} %collective-permute-done.1, f32[1,128,400]{1,0,2:T(1,128)S(1)} %collective-permute-done.2, f32[1,128,400]{1,0,2:T(1,128)S(1)} %collective-permute-done.3, f32[1,128,400]{1,0,2:T(1,128)S(1)} %collective-permute-done.4, f32[1,128,400]{1,0,2:T(1,128)S(1)} %collective-permute-done.5, ...), dimensions={0} | concatenate | bytes 3276800 | tf_op jit(solution)/shard_map/concatenate | solution.py:152
  309.0 110.6 %all-reduce.2.cloned.1.call-done = f32[1345,400]{1,0:T(8,128)} async-done(((f32[1345,400]{1,0:T(8,128)}), f32[1345,400]{1,0:T(8,128)}) %all-reduce.2.cloned.1.call-update) | async-done | bytes 2152016 | tf_op jit(solution)/shard_map/psum | solution.py:131
  421.7 3.8 divide_subtract_fusion
  433.7 6.8 %scatter_custom_fusion.2 = f32[512,400]{1,0:T(8,128)S(1)} fusion(s32[1024]{0:T(1024)S(1)} %bitcast.53, f32[1024,400]{1,0:T(8,128)S(1)} %bitcast.47, f32[]{:T(128)} %constant.118.clone.1), kind=kCustom, calls=%fused_computation.63 | custom fusion | flops 409600 | bytes 819204 | tf_op jit(solution)/shard_map/scatter-add | solution.py:142
  440.6 7.7 %scatter_fusion.1 = f32[512,400]{1,0:T(8,128)S(1)} fusion(f32[512,400]{1,0:T(8,128)S(1)} %scatter_custom_fusion.2, s32[1024]{0:T(1024)S(1)} %bitcast.50, f32[1024,400]{1,0:T(8,128)} %bitcast.43), kind=kCustom, calls=%fused_computation.10 | custom fusion | flops 409600 | bytes 4919296 | tf_op jit(solution)/shard_map/scatter-add | solution.py:155
  (128 shorter events, 73.7 us)
Async XLA Ops:
  8.6 12.5 %copy-start.1 = (f32[512,400]{1,0:T(8,128)}, f32[512,400]{1,0:T(8,128)S(1)}, u32[]{:S(2)}) copy-start(f32[512,400]{1,0:T(8,128)S(1)} %copy.63) | copy-start | bytes 2457604
  14.6 6.5 %copy-start.17 = (s32[1,8,128]{2,1,0:T(8,128)S(1)}, s32[1,8,128]{2,1,0:T(8,128)}, u32[]{:S(2)}) copy-start(s32[1,8,128]{2,1,0:T(8,128)} %param.20) | copy-start | bytes 12292
  14.6 50.3 %all-to-all-start = ((f32[8,128,400]{1,2,0:T(8,128)}), f32[8,128,400]{1,2,0:T(8,128)}, u32[]{:S(2)}, u32[]{:S(2)}) async-start(f32[8,128,400]{1,2,0:T(8,128)} %copy.48), calls=%async_computation | async-start | bytes 3276800 | tf_op jit(solution)/shard_map/all_to_all | solution.py:82
  26.4 38.5 %collective-permute-start = (f32[8,128,400]{1,2,0:T(8,128)}, f32[8,128,400]{1,2,0:T(8,128)}, u32[]{:S(2)}, u32[]{:S(2)}) collective-permute-start(f32[8,128,400]{1,2,0:T(8,128)} %copy.52), channel_id=1, source_target_pairs={{0,24},{8,0},{16,8},{24,16},{1,25},{9,1},{17,9},{25,17},{2,26},{10... | collective-permute-start | bytes 4915208 | tf_op jit(solution)/shard_map/ppermute | solution.py:12
  64.9 44.0 %all-to-all-start.1 = ((f32[8,128,400]{1,2,0:T(8,128)}), f32[8,128,400]{1,2,0:T(8,128)}, u32[]{:S(2)}, u32[]{:S(2)}) async-start(f32[8,128,400]{1,2,0:T(8,128)} %collective-permute-done), calls=%async_computation.1 | async-start | bytes 3276800 | tf_op jit(solution)/shard_map/all_to_all | solution.py:87
  69.6 3.2 copy-start.20
  72.2 5.6 %copy-start.4 = (f32[1345,400]{1,0:T(8,128)}, f32[1345,400]{1,0:T(8,128)S(1)}, u32[]{:S(2)}) copy-start(f32[1345,400]{1,0:T(8,128)S(1)} %copy.50) | copy-start | bytes 6456004
  72.9 4.9 %copy-start.21 = (s32[1024]{0:T(1024)S(1)}, s32[1024]{0:T(1024)}, u32[]{:S(2)}) copy-start(s32[1024]{0:T(1024)} %param.21) | copy-start | bytes 12292
  72.9 4.9 %copy-start.22 = (s32[1024]{0:T(1024)S(1)}, s32[1024]{0:T(1024)}, u32[]{:S(2)}) copy-start(s32[1024]{0:T(1024)} %param.23) | copy-start | bytes 12292
  125.8 6.1 %copy-start.11 = (f32[1024,400]{0,1:T(8,128)S(1)}, f32[1024,400]{0,1:T(8,128)}, u32[]{:S(2)}) copy-start(f32[1024,400]{0,1:T(8,128)} %get-tuple-element.437) | copy-start | bytes 4915204 | tf_op jit(solution)/shard_map/while
  132.8 5.4 %copy-start.6 = (f32[1024,400]{1,0:T(8,128)S(1)}, f32[1024,400]{1,0:T(8,128)}, u32[]{:S(2)}) copy-start(f32[1024,400]{1,0:T(8,128)} %get-tuple-element.453) | copy-start | bytes 4915204 | tf_op jit(solution)/shard_map/while
  159.9 6.1 %copy-start.11 = (f32[1024,400]{0,1:T(8,128)S(1)}, f32[1024,400]{0,1:T(8,128)}, u32[]{:S(2)}) copy-start(f32[1024,400]{0,1:T(8,128)} %get-tuple-element.437) | copy-start | bytes 4915204 | tf_op jit(solution)/shard_map/while
  166.9 5.4 %copy-start.6 = (f32[1024,400]{1,0:T(8,128)S(1)}, f32[1024,400]{1,0:T(8,128)}, u32[]{:S(2)}) copy-start(f32[1024,400]{1,0:T(8,128)} %get-tuple-element.453) | copy-start | bytes 4915204 | tf_op jit(solution)/shard_map/while
  187.6 5.0 %copy-start.23 = (f32[1024]{0:T(1024)}, f32[1024]{0:T(1024)S(1)}, u32[]{:S(2)}) copy-start(f32[1024]{0:T(1024)S(1)} %get-tuple-element.301) | copy-start | bytes 12292
  187.6 3.0 copy-start.7
  206.3 4.5 copy-start
  206.3 225.5 %all-to-all-start.2 = ((f32[8,128,400]{1,2,0:T(8,128)}), f32[8,128,400]{1,2,0:T(8,128)}, u32[]{:S(2)}, u32[]{:S(2)}) async-start(f32[8,128,400]{1,2,0:T(8,128)} %copy.56), calls=%async_computation.2 | async-start | bytes 3276800 | tf_op jit(solution)/shard_map/all_to_all | solution.py:132
  210.8 208.9 %all-reduce.2.cloned.1.call-start = ((), (), s32[]{:S(2)}) async-start(), calls=%async_computation.3 | async-start | bytes 5537792 | tf_op jit(solution)/shard_map/psum | solution.py:131
  233.5 12.1 %collective-permute-start.1 = (f32[1,128,400]{1,0,2:T(1,128)S(1)}, f32[1,128,400]{1,0,2:T(1,128)S(1)}, u32[]{:S(2)}, u32[]{:S(2)}) collective-permute-start(f32[1,128,400]{1,0,2:T(1,128)S(1)} %get-tuple-element.342), channel_id=1, source_target_pairs={{0,7},{1,0},{2,1},{3,2},{4,3},{5,4},{6,5},{7,6},{8,15},{9,8},{10,9... | collective-permute-start | bytes 614408 | tf_op jit(solution)/shard_map/ppermute | solution.py:151
  237.0 19.7 %collective-permute-start.2 = (f32[1,128,400]{1,0,2:T(1,128)S(1)}, f32[1,128,400]{1,0,2:T(1,128)S(1)}, u32[]{:S(2)}, u32[]{:S(2)}) collective-permute-start(f32[1,128,400]{1,0,2:T(1,128)S(1)} %get-tuple-element.341), channel_id=1, source_target_pairs={{0,6},{1,7},{2,0},{3,1},{4,2},{5,3},{6,4},{7,5},{8,14},{9,15},{10,... | collective-permute-start | bytes 614408 | tf_op jit(solution)/shard_map/ppermute | solution.py:151
  237.5 42.4 %collective-permute-start.3 = (f32[1,128,400]{1,0,2:T(1,128)S(1)}, f32[1,128,400]{1,0,2:T(1,128)S(1)}, u32[]{:S(2)}, u32[]{:S(2)}) collective-permute-start(f32[1,128,400]{1,0,2:T(1,128)S(1)} %get-tuple-element.340), channel_id=1, source_target_pairs={{0,5},{1,6},{2,7},{3,0},{4,1},{5,2},{6,3},{7,4},{8,13},{9,14},{10,... | collective-permute-start | bytes 614408 | tf_op jit(solution)/shard_map/ppermute | solution.py:151
  237.6 61.0 %collective-permute-start.4 = (f32[1,128,400]{1,0,2:T(1,128)S(1)}, f32[1,128,400]{1,0,2:T(1,128)S(1)}, u32[]{:S(2)}, u32[]{:S(2)}) collective-permute-start(f32[1,128,400]{1,0,2:T(1,128)S(1)} %get-tuple-element.339), channel_id=1, source_target_pairs={{0,4},{1,5},{2,6},{3,7},{4,0},{5,1},{6,2},{7,3},{8,12},{9,13},{10,... | collective-permute-start | bytes 614408 | tf_op jit(solution)/shard_map/ppermute | solution.py:151
  240.0 58.5 %collective-permute-start.5 = (f32[1,128,400]{1,0,2:T(1,128)S(1)}, f32[1,128,400]{1,0,2:T(1,128)S(1)}, u32[]{:S(2)}, u32[]{:S(2)}) collective-permute-start(f32[1,128,400]{1,0,2:T(1,128)S(1)} %get-tuple-element.338), channel_id=1, source_target_pairs={{0,3},{1,4},{2,5},{3,6},{4,7},{5,0},{6,1},{7,2},{8,11},{9,12},{10,... | collective-permute-start | bytes 614408 | tf_op jit(solution)/shard_map/ppermute | solution.py:151
  245.6 52.9 %collective-permute-start.6 = (f32[1,128,400]{1,0,2:T(1,128)S(1)}, f32[1,128,400]{1,0,2:T(1,128)S(1)}, u32[]{:S(2)}, u32[]{:S(2)}) collective-permute-start(f32[1,128,400]{1,0,2:T(1,128)S(1)} %get-tuple-element.337), channel_id=1, source_target_pairs={{0,2},{1,3},{2,4},{3,5},{4,6},{5,7},{6,0},{7,1},{8,10},{9,11},{10,... | collective-permute-start | bytes 614408 | tf_op jit(solution)/shard_map/ppermute | solution.py:151
  256.7 41.9 %collective-permute-start.7 = (f32[1,128,400]{1,0,2:T(1,128)S(1)}, f32[1,128,400]{1,0,2:T(1,128)S(1)}, u32[]{:S(2)}, u32[]{:S(2)}) collective-permute-start(f32[1,128,400]{1,0,2:T(1,128)S(1)} %get-tuple-element.336), channel_id=1, source_target_pairs={{0,1},{1,2},{2,3},{3,4},{4,5},{5,6},{6,7},{7,0},{8,9},{9,10},{10,1... | collective-permute-start | bytes 614408 | tf_op jit(solution)/shard_map/ppermute | solution.py:151
  305.1 3.8 copy-start.16
  305.2 3.8 copy-start.18
  306.6 115.1 %copy-start.19 = (f32[1345]{0:T(1024)S(1)}, f32[1345]{0:T(1024)}, u32[]{:S(2)}) copy-start(f32[1345]{0:T(1024)} %param.18) | copy-start | bytes 16144
  306.6 115.1 %copy-start.5 = (f32[1345,400]{1,0:T(8,128)S(1)}, f32[1345,400]{1,0:T(8,128)}, u32[]{:S(2)}) copy-start(f32[1345,400]{1,0:T(8,128)} %copy-done.4) | copy-start | bytes 6456004
  306.6 122.4 %collective-permute-start.8 = (f32[8,128,400]{1,2,0:T(8,128)}, f32[8,128,400]{1,2,0:T(8,128)}, u32[]{:S(2)}, u32[]{:S(2)}) collective-permute-start(f32[8,128,400]{1,2,0:T(8,128)} %copy.60), channel_id=1, source_target_pairs={{0,8},{8,16},{16,24},{24,0},{1,9},{9,17},{17,25},{25,1},{2,10},{10... | collective-permute-start | bytes 4915208 | tf_op jit(solution)/shard_map/ppermute | solution.py:12
  440.6 7.9 %copy-start.24 = (f32[512]{0:T(512)S(1)}, f32[512]{0:T(512)}, u32[]{:S(2)}) copy-start(f32[512]{0:T(512)} %param.16) | copy-start | bytes 6148
  440.6 7.9 %copy-start.2 = (f32[512,400]{1,0:T(8,128)S(1)}, f32[512,400]{1,0:T(8,128)}, u32[]{:S(2)}) copy-start(f32[512,400]{1,0:T(8,128)} %copy-done.1) | copy-start | bytes 2457604
  (10 other events, 17.8 us)
Sparse Core Ops, SparseCore 0:
  230.7 188.8 all-reduce.1
